TPU v7x, 32 devices: a whole 2x2x4 slice. The times are simulated.
32 devices in a mesh: fsdp: 32 (over z, y, x, core).
Axes of the slice: x: 2, y: 2, z: 4, core: 2. Of those that a mesh axis runs over, the one named last changes fastest.
Arguments:
- tokens: bfloat16 [4096, 1024], P('fsdp'), may hold values from -160 to 160
- seq_ids: int32 [4096], P('fsdp'), may hold values from 0 to 64, as said below
- grad_output: bfloat16 [4096, 1024], P('fsdp'), may hold values from -6 to 6
- qkv_weight: bfloat16 [3145728], P('fsdp'), may hold values from -0.1875 to 0.1875
- out_weight: bfloat16 [1048576], P('fsdp'), may hold values from -1 to 1
- up_weight: bfloat16 [4194304], P('fsdp'), may hold values from -0.1875 to 0.1875
- down_weight: bfloat16 [4194304], P('fsdp'), may hold values from -0.09375 to 0.09375
- small_params: bfloat16 [12288], P('fsdp'), may hold values from 0.5 to 1.5
Outputs:
- output: bfloat16 [4096, 1024], P('fsdp')
- tokens_grad: bfloat16 [4096, 1024], P('fsdp')
- qkv_weight_grad: float32 [3145728], P('fsdp')
- out_weight_grad: float32 [1048576], P('fsdp')
- up_weight_grad: float32 [4194304], P('fsdp')
- down_weight_grad: float32 [4194304], P('fsdp')
- small_params_grad: float32 [12288], P('fsdp')
Inputs may be any that keep to these rules, and one draw needn't show every extreme that they name: `seq_ids`: within each block of 128 rows the numbers start at 0, rise by one at the first row of each new sequence and never fall; a sequence holds 1 to 64 rows, never crosses a multiple of 64 rows, and every block holds one sequence of exactly 64 rows.
All inputs are finite; a program needn't handle non-finite values.
Results may differ from a plain program's by a relative error of at most 0.012.
The roundings to bfloat16 on the way count: a program that leaves them out, or rounds other values in their place, can miss the bound.
Values may be sent and summed in bfloat16 or wider, within the bound.
A program may use at most 256 MiB of HBM per device.

v0:
```python
import jax
import jax.numpy as jnp
from jax import lax
from jax.sharding import PartitionSpec as P

D = 1024
HEAD_DIM = 64
FF = 4096
TOK_DEV = 128
EPS = 1e-06
ROOT_HALF = 0.7071067811865476
INV_ROOT_TAU = 0.3989422804014327


def matmul(former, latter):
    return jnp.dot(former, latter, preferred_element_type=jnp.float32)


def matmul_tn(former, latter):
    return lax.dot_general(
        former, latter, (((0,), (0,)), ((), ())), preferred_element_type=jnp.float32
    )


def matmul_nt(former, latter):
    return lax.dot_general(
        former, latter, (((1,), (1,)), ((), ())), preferred_element_type=jnp.float32
    )


def unpack(params):
    params = params.astype(jnp.float32)
    bounds = [0, D, 2 * D, 3 * D, 4 * D, 5 * D, 5 * D + FF, 6 * D + FF, 7 * D + FF, 8 * D + FF]
    return [params[bounds[position] : bounds[position + 1]] for position in range(9)]


def shaped(pieces):
    return (
        pieces[0].reshape(D, 3 * D),
        pieces[1].reshape(D, D),
        pieces[2].reshape(D, FF),
        pieces[3].reshape(FF, D),
        pieces[4],
    )


def norm_forward(values, gain, shift):
    center = values - jnp.mean(values, axis=-1, keepdims=True)
    inverse = lax.rsqrt(jnp.mean(center * center, axis=-1, keepdims=True) + EPS)
    normed = center * inverse
    return (normed * gain + shift, normed, inverse)


def norm_backward(upstream, normed, inverse, gain):
    scaled = upstream * gain
    return inverse * (
        scaled
        - jnp.mean(scaled, axis=-1, keepdims=True)
        - normed * jnp.mean(scaled * normed, axis=-1, keepdims=True)
    )


def gelu_curve(values):
    return 0.5 * values * (1.0 + lax.erf(values * ROOT_HALF))


def gelu_slope(values):
    return (
        0.5 * (1.0 + lax.erf(values * ROOT_HALF))
        + values * jnp.exp(-0.5 * values * values) * INV_ROOT_TAU
    )


def split_heads(matrix):
    return matrix.reshape(-1, TOK_DEV, matrix.shape[1] // HEAD_DIM, HEAD_DIM)


def block_mask(ids):
    blocks = ids.reshape(-1, TOK_DEV)
    return (blocks[:, :, None] == blocks[:, None, :])[:, None]


def masked_scores(queries, key_rows, same_seq):
    scores = jnp.einsum(
        "bqhd,bkhd->bhqk",
        split_heads(queries),
        split_heads(key_rows),
        preferred_element_type=jnp.float32,
    ) * HEAD_DIM ** (-0.5)
    return jnp.where(same_seq, scores, -jnp.inf)


def attend(queries, key_rows, value_rows, same_seq):
    scores = masked_scores(queries, key_rows, same_seq)
    row_max = jnp.max(scores, axis=-1, keepdims=True)
    log_total = row_max + jnp.log(jnp.sum(jnp.exp(scores - row_max), axis=-1, keepdims=True))
    attn_probs = jnp.exp(scores - log_total).astype(jnp.bfloat16)
    context = (
        jnp.einsum(
            "bhqk,bkhd->bqhd",
            attn_probs,
            split_heads(value_rows),
            preferred_element_type=jnp.float32,
        )
        .reshape(-1, queries.shape[1])
        .astype(jnp.bfloat16)
    )
    return (context, log_total)


def attend_back(queries, key_rows, value_rows, same_seq, log_total, context_grad):
    columns = queries.shape[1]
    probs_full = jnp.exp(masked_scores(queries, key_rows, same_seq) - log_total)
    probs_bf = probs_full.astype(jnp.bfloat16)
    prob_grad = jnp.einsum(
        "bqhd,bkhd->bhqk",
        split_heads(context_grad),
        split_heads(value_rows),
        preferred_element_type=jnp.float32,
    )
    value_grad = jnp.einsum(
        "bhqk,bqhd->bkhd", probs_bf, split_heads(context_grad), preferred_element_type=jnp.float32
    ).reshape(-1, columns)
    row_delta = jnp.sum(probs_full * prob_grad, axis=-1, keepdims=True)
    score_grad = (probs_full * (prob_grad - row_delta) * HEAD_DIM ** (-0.5)).astype(jnp.bfloat16)
    query_grad = jnp.einsum(
        "bhqk,bkhd->bqhd", score_grad, split_heads(key_rows), preferred_element_type=jnp.float32
    ).reshape(-1, columns)
    key_grad = jnp.einsum(
        "bhqk,bqhd->bkhd", score_grad, split_heads(queries), preferred_element_type=jnp.float32
    ).reshape(-1, columns)
    return (query_grad, key_grad, value_grad)


def forward_pass(tokens, seq_ids, weights):
    qkv_matrix, out_matrix, up_matrix, down_matrix, bias_gain = weights
    (
        query_bias,
        value_bias,
        out_bias,
        gain_one,
        shift_one,
        up_bias,
        down_bias,
        gain_two,
        shift_two,
    ) = unpack(bias_gain)
    same_seq = block_mask(seq_ids)
    projected = matmul(tokens, qkv_matrix)
    queries = (projected[:, :D] + query_bias).astype(jnp.bfloat16)
    key_rows = projected[:, D : 2 * D].astype(jnp.bfloat16)
    value_rows = (projected[:, 2 * D :] + value_bias).astype(jnp.bfloat16)
    context, log_total = attend(queries, key_rows, value_rows, same_seq)
    first_sum = tokens.astype(jnp.float32) + matmul(context, out_matrix) + out_bias
    first_norm, first_unit, first_inv = norm_forward(first_sum, gain_one, shift_one)
    first_bf = first_norm.astype(jnp.bfloat16)
    hidden_pre = matmul(first_bf, up_matrix) + up_bias
    activated = gelu_curve(hidden_pre).astype(jnp.bfloat16)
    second_sum = first_norm + matmul(activated, down_matrix) + down_bias
    result, second_unit, second_inv = norm_forward(second_sum, gain_two, shift_two)
    kept = (
        same_seq,
        queries,
        key_rows,
        value_rows,
        log_total,
        context,
        first_unit,
        first_inv,
        first_bf,
        hidden_pre,
        activated,
        second_unit,
        second_inv,
    )
    return (result.astype(jnp.bfloat16), kept)


def mlp_backward(grad_output, kept, weights):
    qkv_matrix, out_matrix, up_matrix, down_matrix, bias_gain = weights
    gain_two = unpack(bias_gain)[7]
    first_bf, hidden_pre, activated, second_unit, second_inv = (
        kept[8],
        kept[9],
        kept[10],
        kept[11],
        kept[12],
    )
    out_cot = grad_output.astype(jnp.float32)
    gain_two_grad = jnp.sum(out_cot * second_unit, axis=0)
    shift_two_grad = jnp.sum(out_cot, axis=0)
    second_grad = norm_backward(out_cot, second_unit, second_inv, gain_two)
    down_bias_grad = jnp.sum(second_grad, axis=0)
    second_bf = second_grad.astype(jnp.bfloat16)
    down_grad = matmul_tn(activated, second_bf)
    hidden_grad = matmul_nt(second_bf, down_matrix) * gelu_slope(hidden_pre)
    up_bias_grad = jnp.sum(hidden_grad, axis=0)
    hidden_bf = hidden_grad.astype(jnp.bfloat16)
    up_grad = matmul_tn(first_bf, hidden_bf)
    first_grad = second_grad + matmul_nt(hidden_bf, up_matrix)
    return (
        first_grad,
        up_grad,
        down_grad,
        (up_bias_grad, down_bias_grad, gain_two_grad, shift_two_grad),
    )


def attention_backward(tokens, first_grad, kept, weights):
    qkv_matrix, out_matrix, up_matrix, down_matrix, bias_gain = weights
    gain_one = unpack(bias_gain)[3]
    same_seq, queries, key_rows, value_rows, log_total, context, first_unit, first_inv = kept[:8]
    gain_one_grad = jnp.sum(first_grad * first_unit, axis=0)
    shift_one_grad = jnp.sum(first_grad, axis=0)
    residual_grad = norm_backward(first_grad, first_unit, first_inv, gain_one)
    out_bias_grad = jnp.sum(residual_grad, axis=0)
    residual_bf = residual_grad.astype(jnp.bfloat16)
    out_grad = matmul_tn(context, residual_bf)
    context_grad = matmul_nt(residual_bf, out_matrix).astype(jnp.bfloat16)
    query_grad, key_grad, value_grad = attend_back(
        queries, key_rows, value_rows, same_seq, log_total, context_grad
    )
    query_bias_grad = jnp.sum(query_grad, axis=0)
    value_bias_grad = jnp.sum(value_grad, axis=0)
    joined_bf = jnp.concatenate([query_grad, key_grad, value_grad], axis=1).astype(jnp.bfloat16)
    qkv_grad = matmul_tn(tokens, joined_bf)
    tokens_grad = (residual_grad + matmul_nt(joined_bf, qkv_matrix)).astype(jnp.bfloat16)
    return (
        tokens_grad,
        qkv_grad,
        out_grad,
        (query_bias_grad, value_bias_grad, out_bias_grad, gain_one_grad, shift_one_grad),
    )


def shards(
    tokens, seq_ids, grad_output, qkv_weight, out_weight, up_weight, down_weight, small_params
):
    gathered = (
        lax.all_gather(qkv_weight, "fsdp", axis=0, tiled=True),
        lax.all_gather(out_weight, "fsdp", axis=0, tiled=True),
        lax.all_gather(up_weight, "fsdp", axis=0, tiled=True),
        lax.all_gather(down_weight, "fsdp", axis=0, tiled=True),
        lax.all_gather(small_params, "fsdp", axis=0, tiled=True),
    )
    result, kept = forward_pass(tokens, seq_ids, shaped(gathered))
    regained = (
        lax.all_gather(qkv_weight, "fsdp", axis=0, tiled=True),
        lax.all_gather(out_weight, "fsdp", axis=0, tiled=True),
        lax.all_gather(up_weight, "fsdp", axis=0, tiled=True),
        lax.all_gather(down_weight, "fsdp", axis=0, tiled=True),
        lax.all_gather(small_params, "fsdp", axis=0, tiled=True),
    )
    weights = shaped(regained)
    first_grad, up_grad, down_grad, mlp_small = mlp_backward(grad_output, kept, weights)
    tokens_grad, qkv_grad, out_grad, attn_small = attention_backward(
        tokens, first_grad, kept, weights
    )
    small_grad = jnp.concatenate(list(attn_small) + list(mlp_small))
    qkv_share, out_share, up_share, down_share, small_share = (
        lax.psum_scatter(qkv_grad.reshape(-1), "fsdp", scatter_dimension=0, tiled=True),
        lax.psum_scatter(out_grad.reshape(-1), "fsdp", scatter_dimension=0, tiled=True),
        lax.psum_scatter(up_grad.reshape(-1), "fsdp", scatter_dimension=0, tiled=True),
        lax.psum_scatter(down_grad.reshape(-1), "fsdp", scatter_dimension=0, tiled=True),
        lax.psum_scatter(small_grad, "fsdp", scatter_dimension=0, tiled=True),
    )
    return (result, tokens_grad, qkv_share, out_share, up_share, down_share, small_share)


def solution(mesh):
    in_specs = (
        P("fsdp", None),
        P("fsdp"),
        P("fsdp", None),
        P("fsdp"),
        P("fsdp"),
        P("fsdp"),
        P("fsdp"),
        P("fsdp"),
    )
    out_specs = (
        P("fsdp", None),
        P("fsdp", None),
        P("fsdp"),
        P("fsdp"),
        P("fsdp"),
        P("fsdp"),
        P("fsdp"),
    )
    return jax.shard_map(shards, mesh=mesh, in_specs=in_specs, out_specs=out_specs, check_vma=False)
```

profile of v0, /device:TPU:0, one launch (start us, length us, event | category | flops | bytes accessed | tf_op | source)
XLA Modules:
  0.0 1156.3 jit_solution(16009765625532053074)
XLA Ops:
  7.2 0.7 all-gather.8.cloned.1.call-update
  7.9 0.7 all-gather.6.cloned.1.call-update
  8.7 0.7 all-gather.10.cloned.1.call-update
  9.4 0.5 all-gather.12.cloned.1.call-update
  10.0 0.7 reshape.250
  10.7 43.4 %all-gather = bf16[32,1,384]{2,1,0:T(2,128)(2,1)S(1)} all-gather(bf16[1,1,384]{2,1,0:T(2,128)(2,1)S(1)} %reshape.250), channel_id=1, replica_groups=mesh['fsdp'=32] {'fsdp'}, dimensions={0}, use_global_device_ids=true | all-gather | bytes 25344 | tf_op jit(solution)/shard_map/all_gather | solution.py:244
  54.1 0.8 broadcast_compare_fusion
  55.0 14.9 %all-gather.8.cloned.1.call-done = bf16[1048576]{0:T(1024)(128)(2,1)} async-done(((bf16[32768]{0:T(1024)(128)(2,1)}), bf16[1048576]{0:T(1024)(128)(2,1)}) %all-gather.8.cloned.1.call-update) | async-done | bytes 2097168 | tf_op jit(solution)/shard_map/all_gather | solution.py:241
  69.8 2.8 reshape.239
  72.7 68.1 %all-gather.6.cloned.1.call-done = bf16[3145728]{0:T(1024)(128)(2,1)} async-done(((bf16[98304]{0:T(1024)(128)(2,1)}), bf16[3145728]{0:T(1024)(128)(2,1)}) %all-gather.6.cloned.1.call-update) | async-done | bytes 6291472 | tf_op jit(solution)/shard_map/all_gather | solution.py:240
  140.7 10.3 reshape.235
  151.0 3.8 fusion.63
  155.6 0.4 fusion.57
  156.1 0.3 convolution_convert_fusion.2
  156.5 0.5 fusion.58
  157.2 62.0 %all-gather.10.cloned.1.call-done = bf16[4194304]{0:T(1024)(128)(2,1)} async-done(((bf16[131072]{0:T(1024)(128)(2,1)}), bf16[4194304]{0:T(1024)(128)(2,1)}) %all-gather.10.cloned.1.call-update) | async-done | bytes 8388624 | tf_op jit(solution)/shard_map/all_gather | solution.py:242
  219.2 13.4 %reshape.240 = bf16[1024,4096]{1,0:T(8,128)(2,1)} reshape(bf16[4194304]{0:T(1024)(128)(2,1)} %all-gather.10.cloned.1.call-done) | data formatting | bytes 16777216 | tf_op jit(solution)/shard_map/reshape | solution.py:41
  232.6 4.8 convolution_add_fusion
  237.3 60.3 %all-gather.12.cloned.1.call-done = bf16[4194304]{0:T(1024)(128)(2,1)} async-done(((bf16[131072]{0:T(1024)(128)(2,1)}), bf16[4194304]{0:T(1024)(128)(2,1)}) %all-gather.12.cloned.1.call-update) | async-done | bytes 8388624 | tf_op jit(solution)/shard_map/all_gather | solution.py:243
  297.6 13.3 %reshape.241 = bf16[4096,1024]{1,0:T(8,128)(2,1)} reshape(bf16[4194304]{0:T(1024)(128)(2,1)} %all-gather.12.cloned.1.call-done) | data formatting | bytes 16777216 | tf_op jit(solution)/shard_map/reshape | solution.py:42
  310.9 5.0 fusion.59
  316.5 1.0 fusion.51
  317.4 3.5 fusion.62
  321.0 3.0 multiply_reduce_fusion.1
  324.3 0.8 copy-done.3
  325.0 1.5 convolution_convert_fusion.1
  326.6 1.8 copy.40
  328.4 2.5 fusion.54
  330.9 2.4 fusion.64
  333.2 3.7 convolution_convert_fusion
  336.9 3.7 fusion.55
  340.6 1.8 convolution_bitcast_fusion.3
  342.4 8.1 convolution_bitcast_fusion
  350.5 8.2 convolution_bitcast_fusion.1
  358.7 3.0 copy.50
  361.7 6.5 convolution_bitcast_fusion.2
  368.2 12.6 %copy.44 = f32[1024,3072]{1,0:T(8,128)} copy(f32[1024,3072]{0,1:T(8,128)} %convolution_bitcast_fusion.2) | data formatting | bytes 25165824 | tf_op jit(solution)/shard_map/dot_general | solution.py:20
  380.7 12.0 %copy.49 = f32[128,24,8,128]{3,1,2,0:T(8,128)} copy(f32[128,24,8,128]{3,2,1,0:T(8,128)} %bitcast.66) | data formatting | bytes 25165824
  392.8 14.1 %copy.52 = f32[512,8,8,128]{3,1,2,0:T(8,128)} copy(f32[512,8,8,128]{3,2,1,0:T(8,128)} %convolution_bitcast_fusion) | data formatting | bytes 33554432
  406.9 14.1 %copy.51 = f32[128,32,8,128]{3,1,2,0:T(8,128)} copy(f32[128,32,8,128]{3,2,1,0:T(8,128)} %convolution_bitcast_fusion.1) | data formatting | bytes 33554432
  421.2 41.5 %all-reduce.4 = f32[12288]{0:T(1024)S(1)} all-reduce(f32[12288]{0:T(1024)S(1)} %constant_dynamic-update-slice_fusion), channel_id=6, replica_groups=mesh['fsdp'=32] {'fsdp'}, use_global_device_ids=true, to_apply=%region_24.25.clone | all-reduce | flops 12288 | bytes 98304
  462.7 0.7 dynamic-slice.4
  463.4 5.9 fusion.12
  469.3 673.4 %all-reduce.8.cloned.1.call-done = (f32[3145728]{0:T(1024)}, f32[1048576]{0:T(1024)}, f32[4194304]{0:T(1024)}, f32[4194304]{0:T(1024)}) async-done(((f32[3145728]{0:T(1024)}, f32[1048576]{0:T(1024)}, f32[4194304]{0:T(1024)}, f32[4194304]{0:T(1024)}), (f32[3145728]{0:T(1024)}, f32[1048576]{0:T(1024)}, f32[4194304]{0:T(1024)}, f32[4194304]{0:T(1024)})) %all-reduce.8.cloned.1.call-update) | async-done | bytes 50331664
  1142.7 1.9 dynamic-slice.2
  1144.5 1.9 dynamic-slice.3
  1146.4 1.8 dynamic-slice
  1148.2 1.6 dynamic-slice.1
  (79 shorter events, 2.2 us)
Async XLA Ops:
  7.2 62.6 %all-gather.8.cloned.1.call-start = ((), (), s32[]{:S(2)}) async-start(), calls=%async_computation.1 | async-start | bytes 2162688 | tf_op jit(solution)/shard_map/all_gather | solution.py:241
  7.9 132.8 %all-gather.6.cloned.1.call-start = ((), (), s32[]{:S(2)}) async-start(), calls=%async_computation | async-start | bytes 6488064 | tf_op jit(solution)/shard_map/all_gather | solution.py:240
  8.6 210.5 %all-gather.10.cloned.1.call-start = ((), (), s32[]{:S(2)}) async-start(), calls=%async_computation.2 | async-start | bytes 8650752 | tf_op jit(solution)/shard_map/all_gather | solution.py:242
  9.4 288.2 %all-gather.12.cloned.1.call-start = ((), (), s32[]{:S(2)}) async-start(), calls=%async_computation.3 | async-start | bytes 8650752 | tf_op jit(solution)/shard_map/all_gather | solution.py:243
  10.0 1132.7 %all-reduce.8.cloned.1.call-start = ((), (), s32[]{:S(2)}) async-start(), calls=%async_computation.4 | async-start | bytes 100663296
  72.6 83.8 %copy-start = (bf16[1024,1024]{1,0:T(8,128)(2,1)}, bf16[1024,1024]{1,0:T(8,128)(2,1)S(1)}, u32[]{:S(2)}) copy-start(bf16[1024,1024]{1,0:T(8,128)(2,1)S(1)} %reshape.239) | copy-start | bytes 6291460
  72.6 78.4 %copy-start.7 = (bf16[128,1024]{1,0:T(8,128)(2,1)S(1)}, bf16[128,1024]{1,0:T(8,128)(2,1)}, u32[]{:S(2)}) copy-start(bf16[128,1024]{1,0:T(8,128)(2,1)} %param.8) | copy-start | bytes 786436
  155.2 0.9 copy-start.13
  155.4 1.1 copy-start.12
  155.5 0.9 copy-start.8
  155.9 1.1 copy-start.2
  156.4 76.1 %copy-start.9 = (bf16[16,64,128]{2,1,0:T(8,128)(2,1)}, bf16[16,64,128]{2,1,0:T(8,128)(2,1)S(1)}, u32[]{:S(2)}) copy-start(bf16[16,64,128]{2,1,0:T(8,128)(2,1)S(1)} %convolution_convert_fusion.2) | copy-start | bytes 786436
  310.9 6.5 slice-start.2
  310.9 5.3 copy-start.11
  310.9 6.5 slice-start.3
  316.5 4.5 slice-start
  317.4 3.5 slice-start.1
  320.9 3.1 copy-start.5
  320.9 4.1 copy-start.1
  324.2 0.8 copy-start.3
  342.4 8.1 copy-start.6
  358.7 3.0 copy-start.10
  358.7 3.0 copy-start.14
  358.7 3.0 copy-start.15
  421.0 42.4 %copy-start.4 = (f32[128,1024]{1,0:T(8,128)S(1)}, f32[128,1024]{1,0:T(8,128)}, u32[]{:S(2)}) copy-start(f32[128,1024]{1,0:T(8,128)} %copy-done.3) | copy-start | bytes 1572868
Sparse Core Ops, SparseCore 0:
  10.8 58.9 all-gather.7
  72.7 67.9 all-gather.5
  143.6 75.5 all-gather.9
  221.9 75.6 all-gather.11
  421.1 721.5 all-reduce.7
where the time goes:
time: 1160 us
  waiting for transfers between devices  881 us (76%)
  local copies, waits for them, and re-layouts  107 us (9%)
  blocking collectives  84.9 us (7%)
  matrix products  65.5 us (6%)
  between operations  14.2 us (1%)
    unnamed x6, waiting for transfers between devices  676 us
    all_gather x1, waiting for transfers between devices, shards(): lax.all_gather(qkv_weight, 'fsdp', axis=0, tiled=True)  68.1 us
    all_gather x1, waiting for transfers between devices, shards(): lax.all_gather(up_weight, 'fsdp', axis=0, tiled=True)  62 us
    all_gather x1, waiting for transfers between devices, shards(): lax.all_gather(down_weight, 'fsdp', axis=0, tiled=True)  60.3 us
    unnamed x58, local copies, waits for them, and re-layouts  52.5 us
    all_gather x1, blocking collectives, shards(): lax.all_gather(small_params, 'fsdp', axis=0, tiled=True)  43.4 us
    unnamed x1, blocking collectives  41.5 us
    dot_general x4, matrix products, matmul_tn(): lax.dot_general(former, latter, (((0,), (0,)), ((), ())), preferred_eleme...  24.6 us
  transfers between devices with their start and end apart: 5, of which 5 were waited for; matrix products, arithmetic and copies ran while one was open for 4% of the time, Pallas kernels for 0%

commit v1 on v0

--- a/solution.py
+++ b/solution.py
@@ -1,3 +1,4 @@
+import functools
 import jax
 import jax.numpy as jnp
 from jax import lax
@@ -10,6 +11,23 @@
 EPS = 1e-06
 ROOT_HALF = 0.7071067811865476
 INV_ROOT_TAU = 0.3989422804014327
+
+
+def produce_the_array(my_tile, link_axis):
+    state_now = lax.axis_size(link_axis)
+    work_now, u1, val2 = (state_now, lax.axis_index(link_axis), my_tile.shape[0])
+    upper, long_array = (my_tile, 1)
+    while long_array < work_now:
+        z = lax.ppermute(
+            upper, link_axis, [(no, (no - long_array) % work_now) for no in range(work_now)]
+        )
+        upper = jnp.concatenate([upper, z], axis=0)
+        long_array = 2 * long_array
+    even = jnp.roll(upper, shift=u1 * val2, axis=0)
+    return even
+
+
+keep_up_the_sectors = functools.partial(produce_the_array, link_axis="fsdp")
 
 
 def matmul(former, latter):
@@ -240,7 +258,7 @@
         lax.all_gather(qkv_weight, "fsdp", axis=0, tiled=True),
         lax.all_gather(out_weight, "fsdp", axis=0, tiled=True),
         lax.all_gather(up_weight, "fsdp", axis=0, tiled=True),
-        lax.all_gather(down_weight, "fsdp", axis=0, tiled=True),
+        keep_up_the_sectors(down_weight),
         lax.all_gather(small_params, "fsdp", axis=0, tiled=True),
     )
     result, kept = forward_pass(tokens, seq_ids, shaped(gathered))

time: 1160 us -> 1390 us (1.20)
  blocking collectives: 84.9 us -> 170 us
  waiting for transfers between devices: 881 us -> 966 us
  local copies, waits for them, and re-layouts: 107 us -> 148 us
  starting transfers between devices: 0.19 us -> 14.3 us
    ppermute x0 -> x5, waiting for transfers between devices: none -> 135 us  [produce_the_array(): lax.ppermute(upper, link_axis, [(no, (no - long_array) % work_now) for no...]
    all_gather x1, blocking collectives: 43.4 us -> 129 us  [shards(): lax.all_gather(small_params, 'fsdp', axis=0, tiled=True)]
    all_gather x1, waiting for transfers between devices: 68.1 us -> 39.8 us  [shards(): lax.all_gather(qkv_weight, 'fsdp', axis=0, tiled=True)]
    all_gather x1, waiting for transfers between devices: 14.9 us -> 0.02 us  [shards(): lax.all_gather(out_weight, 'fsdp', axis=0, tiled=True)]
    unnamed x58 -> x80, local copies, waits for them, and re-layouts: 52.5 us -> 66.9 us
    ppermute x0 -> x5, starting transfers between devices: none -> 14.1 us  [produce_the_array(): lax.ppermute(upper, link_axis, [(no, (no - long_array) % work_now) for no...]
  transfers between devices with their start and end apart: 5 -> 10, of which waited for: 5 -> 9; matrix products, arithmetic and copies ran while one was open for 4% -> 7% of each run, Pallas kernels for 0% -> 0%
where the time goes in v1:
time: 1390 us
  waiting for transfers between devices  966 us (69%)
  blocking collectives  170 us (12%)
  local copies, waits for them, and re-layouts  148 us (11%)
  matrix products  72.3 us (5%)
  starting transfers between devices  14.3 us (1%)
  between operations  14.3 us (1%)
    unnamed x6, waiting for transfers between devices  675 us
    ppermute x5, waiting for transfers between devices, produce_the_array(): lax.ppermute(upper, link_axis, [(no, (no - long_array) % work_now) for no...  135 us
    all_gather x1, blocking collectives, shards(): lax.all_gather(small_params, 'fsdp', axis=0, tiled=True)  129 us
    unnamed x80, local copies, waits for them, and re-layouts  66.9 us
    all_gather x1, waiting for transfers between devices, shards(): lax.all_gather(up_weight, 'fsdp', axis=0, tiled=True)  62 us
    all_gather x1, waiting for transfers between devices, shards(): lax.all_gather(down_weight, 'fsdp', axis=0, tiled=True)  53.8 us
    unnamed x1, blocking collectives  41.7 us
    all_gather x1, waiting for transfers between devices, shards(): lax.all_gather(qkv_weight, 'fsdp', axis=0, tiled=True)  39.8 us
  transfers between devices with their start and end apart: 10, of which 9 were waited for; matrix products, arithmetic and copies ran while one was open for 7% of the time, Pallas kernels for 0%

profile of v1, /device:TPU:0, one launch (start us, length us, event | category | flops | bytes accessed | tf_op | source)
XLA Modules:
  0.0 1389.7 jit_solution(3934887615424369426)
XLA Ops:
  8.7 6.5 collective-permute-start
  15.2 1.8 constant_dynamic-update-slice_fusion
  17.0 2.4 collective-permute-done
  21.9 10.3 collective-permute-done.1
  35.4 23.2 %collective-permute-done.2 = bf16[524288]{0:T(1024)(128)(2,1)S(1)} collective-permute-done((bf16[524288]{0:T(1024)(128)(2,1)S(1)}, bf16[524288]{0:T(1024)(128)(2,1)S(1)}, u32[]{:S(2)}, u32[]{:S(2)}) %collective-permute-start.2) | collective-permute-done | bytes 1048608 | tf_op jit(solution)/shard_map/ppermute | solution.py:21
  58.8 4.5 collective-permute-start.3
  64.8 43.9 %collective-permute-done.3 = bf16[1048576]{0:T(1024)(128)(2,1)S(1)} collective-permute-done((bf16[1048576]{0:T(1024)(128)(2,1)S(1)}, bf16[1048576]{0:T(1024)(128)(2,1)S(1)}, u32[]{:S(2)}, u32[]{:S(2)}) %collective-permute-start.3) | collective-permute-done | bytes 2097184 | tf_op jit(solution)/shard_map/ppermute | solution.py:21
  110.0 2.2 constant_dynamic-update-slice_fusion.3
  113.9 128.6 %all-gather = bf16[32,1,384]{2,1,0:T(2,128)(2,1)S(1)} all-gather(bf16[1,1,384]{2,1,0:T(2,128)(2,1)S(1)} %reshape.253), channel_id=1, replica_groups=mesh['fsdp'=32] {'fsdp'}, dimensions={0}, use_global_device_ids=true | all-gather | bytes 25344 | tf_op jit(solution)/shard_map/all_gather | solution.py:262
  242.7 2.8 reshape.241
  245.6 55.6 %collective-permute-done.4 = bf16[2097152]{0:T(1024)(128)(2,1)} collective-permute-done((bf16[2097152]{0:T(1024)(128)(2,1)}, bf16[2097152]{0:T(1024)(128)(2,1)}, u32[]{:S(2)}, u32[]{:S(2)}) %collective-permute-start.4) | collective-permute-done | bytes 4194336 | tf_op jit(solution)/shard_map/ppermute | solution.py:21
  301.2 3.8 constant_dynamic-update-slice_fusion.17
  309.8 3.7 constant_dynamic-update-slice_fusion.11
  313.5 7.1 dynamic_slice.4
  320.6 13.4 reshape.243
  333.9 39.8 %all-gather.6.cloned.1.call-done = bf16[3145728]{0:T(1024)(128)(2,1)} async-done(((bf16[98304]{0:T(1024)(128)(2,1)}), bf16[3145728]{0:T(1024)(128)(2,1)}) %all-gather.6.cloned.1.call-update) | async-done | bytes 6291472 | tf_op jit(solution)/shard_map/all_gather | solution.py:258
  373.8 10.3 reshape.237
  384.1 3.8 fusion.63
  390.3 62.0 %all-gather.10.cloned.1.call-done = bf16[4194304]{0:T(1024)(128)(2,1)} async-done(((bf16[131072]{0:T(1024)(128)(2,1)}), bf16[4194304]{0:T(1024)(128)(2,1)}) %all-gather.10.cloned.1.call-update) | async-done | bytes 8388624 | tf_op jit(solution)/shard_map/all_gather | solution.py:260
  452.3 13.4 reshape.242
  465.6 4.8 convolution_add_fusion
  470.4 5.0 fusion.59
  476.9 53.8 %all-gather.12.cloned.1.call-done = bf16[4194304]{0:T(1024)(128)(2,1)} async-done(((bf16[131072]{0:T(1024)(128)(2,1)}), bf16[4194304]{0:T(1024)(128)(2,1)}) %all-gather.12.cloned.1.call-update) | async-done | bytes 8388624 | tf_op jit(solution)/shard_map/all_gather | solution.py:269
  530.7 13.3 reshape.244
  544.0 6.5 fusion.62
  550.5 6.8 multiply_reduce_fusion.1
  558.4 1.5 convolution_convert_fusion.1
  559.9 1.8 copy.40
  561.7 2.5 fusion.54
  564.2 2.4 fusion.64
  566.6 3.7 convolution_convert_fusion
  570.3 3.7 fusion.55
  574.0 1.8 convolution_bitcast_fusion.3
  575.8 8.1 convolution_bitcast_fusion
  583.9 8.4 convolution_bitcast_fusion.1
  592.3 3.0 copy.50
  595.3 6.3 convolution_bitcast_fusion.2
  601.6 12.6 copy.44
  614.2 12.0 copy.49
  626.2 14.1 %copy.52 = f32[512,8,8,128]{3,1,2,0:T(8,128)} copy(f32[512,8,8,128]{3,2,1,0:T(8,128)} %convolution_bitcast_fusion) | data formatting | bytes 33554432
  640.3 14.1 %copy.51 = f32[128,32,8,128]{3,1,2,0:T(8,128)} copy(f32[128,32,8,128]{3,2,1,0:T(8,128)} %convolution_bitcast_fusion.1) | data formatting | bytes 33554432
  654.6 41.7 %all-reduce.4 = f32[12288]{0:T(1024)S(1)} all-reduce(f32[12288]{0:T(1024)S(1)} %constant_dynamic-update-slice_fusion.18), channel_id=6, replica_groups=mesh['fsdp'=32] {'fsdp'}, use_global_device_ids=true, to_apply=%region_24.25.clone | all-reduce | flops 12288 | bytes 98304
  697.0 5.9 fusion.12
  703.0 673.2 %all-reduce.8.cloned.1.call-done = (f32[3145728]{0:T(1024)}, f32[1048576]{0:T(1024)}, f32[4194304]{0:T(1024)}, f32[4194304]{0:T(1024)}) async-done(((f32[3145728]{0:T(1024)}, f32[1048576]{0:T(1024)}, f32[4194304]{0:T(1024)}, f32[4194304]{0:T(1024)}), (f32[3145728]{0:T(1024)}, f32[1048576]{0:T(1024)}, f32[4194304]{0:T(1024)}, f32[4194304]{0:T(1024)})) %all-reduce.8.cloned.1.call-update) | async-done | bytes 50331664
  1376.1 1.9 dynamic-slice.2
  1378.0 1.9 dynamic-slice.3
  1379.9 1.8 dynamic-slice
  1381.6 1.6 dynamic-slice.1
  (116 shorter events, 22.4 us)
Async XLA Ops:
  7.2 51.5 %copy-start.3 = (bf16[131072]{0:T(1024)(128)(2,1)S(1)}, bf16[131072]{0:T(1024)(128)(2,1)}, u32[]{:S(2)}) copy-start(bf16[131072]{0:T(1024)(128)(2,1)} %param.14) | copy-start | bytes 786436
  7.2 235.5 %all-gather.8.cloned.1.call-start = ((), (), s32[]{:S(2)}) async-start(), calls=%async_computation.1 | async-start | bytes 2162688 | tf_op jit(solution)/shard_map/all_gather | solution.py:259
  7.9 365.9 %all-gather.6.cloned.1.call-start = ((), (), s32[]{:S(2)}) async-start(), calls=%async_computation | async-start | bytes 6488064 | tf_op jit(solution)/shard_map/all_gather | solution.py:258
  8.7 443.6 %all-gather.10.cloned.1.call-start = ((), (), s32[]{:S(2)}) async-start(), calls=%async_computation.2 | async-start | bytes 8650752 | tf_op jit(solution)/shard_map/all_gather | solution.py:260
  8.7 10.7 collective-permute-start
  15.2 515.5 %all-gather.12.cloned.1.call-start = ((), (), s32[]{:S(2)}) async-start(), calls=%async_computation.3 | async-start | bytes 8650752 | tf_op jit(solution)/shard_map/all_gather | solution.py:269
  19.4 39.5 %copy-start.9 = (bf16[131072]{0:T(1024)(128)(2,1)}, bf16[131072]{0:T(1024)(128)(2,1)S(1)}, u32[]{:S(2)}) copy-start(bf16[131072]{0:T(1024)(128)(2,1)S(1)} %collective-permute-done) | copy-start | bytes 786436
  20.4 11.7 collective-permute-start.1
  32.2 26.5 %copy-start.7 = (bf16[262144]{0:T(1024)(128)(2,1)}, bf16[262144]{0:T(1024)(128)(2,1)S(1)}, u32[]{:S(2)}) copy-start(bf16[262144]{0:T(1024)(128)(2,1)S(1)} %collective-permute-done.1) | copy-start | bytes 1572868
  33.4 25.3 %collective-permute-start.2 = (bf16[524288]{0:T(1024)(128)(2,1)S(1)}, bf16[524288]{0:T(1024)(128)(2,1)S(1)}, u32[]{:S(2)}, u32[]{:S(2)}) collective-permute-start(bf16[524288]{0:T(1024)(128)(2,1)S(1)} %pad_maximum_fusion.1), channel_id=1, source_target_pairs={{0,28},{1,29},{2,30},{3,31},{4,0},{5,1},{6,2},{7,3},{8,4},{9,5},{1... | collective-permute-start | bytes 3145736 | tf_op jit(solution)/shard_map/ppermute | solution.py:21
  58.8 49.9 %collective-permute-start.3 = (bf16[1048576]{0:T(1024)(128)(2,1)S(1)}, bf16[1048576]{0:T(1024)(128)(2,1)S(1)}, u32[]{:S(2)}, u32[]{:S(2)}) collective-permute-start(bf16[1048576]{0:T(1024)(128)(2,1)S(1)} %pad_maximum_fusion), channel_id=1, source_target_pairs={{0,24},{1,25},{2,26},{3,27},{4,28},{5,29},{6,30},{7,31},{8,0},{9,1... | collective-permute-start | bytes 6291464 | tf_op jit(solution)/shard_map/ppermute | solution.py:21
  63.3 50.5 %copy-start.25 = (bf16[384]{0:T(512)(128)(2,1)S(1)}, bf16[384]{0:T(512)(128)(2,1)}, u32[]{:S(2)}) copy-start(bf16[384]{0:T(512)(128)(2,1)} %param.15) | copy-start | bytes 2308
  63.3 179.2 %copy-start.24 = (s32[128]{0:T(128)S(1)}, s32[128]{0:T(128)}, u32[]{:S(2)}) copy-start(s32[128]{0:T(128)} %param.9) | copy-start | bytes 1540
  108.7 1.3 copy-start.5
  112.3 188.9 %collective-permute-start.4 = (bf16[2097152]{0:T(1024)(128)(2,1)}, bf16[2097152]{0:T(1024)(128)(2,1)}, u32[]{:S(2)}, u32[]{:S(2)}) collective-permute-start(bf16[2097152]{0:T(1024)(128)(2,1)} %get-tuple-element.23), channel_id=1, source_target_pairs={{0,16},{1,17},{2,18},{3,19},{4,20},{5,21},{6,22},{7,23},{8,24},{9,... | collective-permute-start | bytes 12582920 | tf_op jit(solution)/shard_map/ppermute | solution.py:21
  113.8 1262.3 %all-reduce.8.cloned.1.call-start = ((), (), s32[]{:S(2)}) async-start(), calls=%async_computation.4 | async-start | bytes 100663296
  245.5 144.0 %copy-start = (bf16[1024,1024]{1,0:T(8,128)(2,1)}, bf16[1024,1024]{1,0:T(8,128)(2,1)S(1)}, u32[]{:S(2)}) copy-start(bf16[1024,1024]{1,0:T(8,128)(2,1)S(1)} %reshape.241) | copy-start | bytes 6291460
  301.1 3.8 copy-start.4
  301.2 4.5 copy-start.10
  301.2 5.2 copy-start.8
  304.9 3.4 copy-start.6
  333.9 50.2 %copy-start.15 = (bf16[128,1024]{1,0:T(8,128)(2,1)S(1)}, bf16[128,1024]{1,0:T(8,128)(2,1)}, u32[]{:S(2)}) copy-start(bf16[128,1024]{1,0:T(8,128)(2,1)} %param.8) | copy-start | bytes 786436
  388.3 0.9 copy-start.21
  388.5 1.1 copy-start.20
  388.6 0.9 copy-start.16
  389.0 1.1 copy-start.2
  389.5 76.1 %copy-start.17 = (bf16[16,64,128]{2,1,0:T(8,128)(2,1)}, bf16[16,64,128]{2,1,0:T(8,128)(2,1)S(1)}, u32[]{:S(2)}) copy-start(bf16[16,64,128]{2,1,0:T(8,128)(2,1)S(1)} %convolution_convert_fusion.2) | copy-start | bytes 786436
  470.4 5.2 copy-start.19
  550.5 6.9 copy-start.13
  550.5 7.9 copy-start.1
  557.6 0.8 copy-start.11
  575.8 8.1 copy-start.14
  592.3 3.0 copy-start.18
  592.3 3.0 copy-start.22
  592.3 3.0 copy-start.23
  654.4 42.6 %copy-start.12 = (f32[128,1024]{1,0:T(8,128)S(1)}, f32[128,1024]{1,0:T(8,128)}, u32[]{:S(2)}) copy-start(f32[128,1024]{1,0:T(8,128)} %copy-done.11) | copy-start | bytes 1572868
Sparse Core Ops, SparseCore 0:
  10.8 207.0 all-gather.7
  220.8 152.9 all-gather.5
  376.7 75.5 all-gather.9
  455.0 75.6 all-gather.11
  654.6 721.5 all-reduce.7
